TPU v7x, 32 devices: a whole 2x2x4 slice. The times are simulated.
32 devices in a mesh: dp: 4 (over y, x), mp: 8 (over z, core).
Axes of the slice: x: 2, y: 2, z: 4, core: 2. Of those that a mesh axis runs over, the one named last changes fastest.
Arguments:
- tokens: bfloat16 [512, 6144], P(('dp', 'mp')), may hold values from -6 to 6
- norm_gain: float32 [6144], replicated, may hold values from 0.5 to 1.5
- up_weight: bfloat16 [6144, 16384], P(None, 'mp'), may hold values from -0.078125 to 0.078125
- down_weight: bfloat16 [16384, 6144], P('mp'), may hold values from -0.046875 to 0.046875
- out_grad: bfloat16 [512, 6144], P(('dp', 'mp')), may hold values from -6 to 6
Outputs:
- input_grad: bfloat16 [512, 6144], P(('dp', 'mp'))
- up_grad: bfloat16 [6144, 16384], P('dp', 'mp')
- down_grad: bfloat16 [16384, 6144], P('mp', 'dp')
- gain_grad: float32 [6144], replicated
All inputs are finite; a program needn't handle non-finite values.
Results may differ from a plain program's by a relative error of at most 0.018.
Values may be sent and summed in bfloat16 or wider, within the bound.
No kernel may reach another device: no remote copies, remote signals or barrier semaphores. Data moves between devices by JAX's collectives and lax.ppermute only.
A program may use at most 192 MiB of HBM per device.

v0:
```python
import math
import jax
import jax.numpy as jnp
from jax import lax
from jax.sharding import PartitionSpec as P


def gelu_value(preact):
    return 0.5 * preact * (1.0 + lax.erf(preact * 0.7071067811865476))


def gelu_slope(preact):
    return (
        0.5 * (1.0 + lax.erf(preact * 0.7071067811865476))
        + preact * jnp.exp(-0.5 * preact * preact) * 0.3989422804014327
    )


def per_device(tokens, norm_gain, up_weight, down_weight, out_grad):
    values = tokens.astype(jnp.float32)
    centered = values - jnp.mean(values, axis=1, keepdims=True)
    inv_std = lax.rsqrt(jnp.mean(centered * centered, axis=1, keepdims=True) + 1e-06)
    x_hat = centered * inv_std
    normed = (x_hat * norm_gain).astype(jnp.bfloat16)
    normed_all, cotan_all = (
        lax.all_gather(normed, "mp", axis=0, tiled=True),
        lax.all_gather(out_grad, "mp", axis=0, tiled=True),
    )
    preact = jnp.dot(normed_all, up_weight, preferred_element_type=jnp.float32)
    hidden = gelu_value(preact).astype(jnp.bfloat16)
    hid_grad = lax.dot_general(
        cotan_all, down_weight, (((1,), (1,)), ((), ())), preferred_element_type=jnp.float32
    )
    pre_grad = (hid_grad * gelu_slope(preact)).astype(jnp.bfloat16)
    norm_grad = lax.psum_scatter(
        lax.dot_general(
            pre_grad, up_weight, (((1,), (1,)), ((), ())), preferred_element_type=jnp.float32
        ),
        "mp",
        scatter_dimension=0,
        tiled=True,
    )
    replicas = lax.axis_size("dp")
    group = normed_all.shape[0]
    factor = 1.0 / math.sqrt(group * replicas)
    gain_grad = lax.psum(jnp.sum(norm_grad * x_hat, axis=0), ("dp", "mp")) * factor
    scaled = norm_gain * norm_grad
    input_grad = (
        scaled
        - jnp.mean(scaled, axis=1, keepdims=True)
        - x_hat * jnp.mean(scaled * x_hat, axis=1, keepdims=True)
    ) * inv_std
    normed_cols, cotan_cols = (
        lax.all_to_all(normed_all, "dp", split_axis=1, concat_axis=0, tiled=True),
        lax.all_to_all(cotan_all, "dp", split_axis=1, concat_axis=0, tiled=True),
    )
    hidden_all, pre_all = (
        lax.all_gather(hidden, "dp", axis=0, tiled=True),
        lax.all_gather(pre_grad, "dp", axis=0, tiled=True),
    )

    def stacked(array):
        return array.reshape(replicas, group, array.shape[1])

    up_parts = jnp.einsum(
        "rtk,rtf->rkf", stacked(normed_cols), stacked(pre_all), preferred_element_type=jnp.float32
    )
    down_parts = jnp.einsum(
        "rtf,rtk->rfk", stacked(hidden_all), stacked(cotan_cols), preferred_element_type=jnp.float32
    )
    up_total = jnp.sum(up_parts.astype(jnp.bfloat16).astype(jnp.float32), axis=0)
    down_total = jnp.sum(down_parts.astype(jnp.bfloat16).astype(jnp.float32), axis=0)
    up_grad = (up_total * factor).astype(jnp.bfloat16)
    down_grad = (down_total * factor).astype(jnp.bfloat16)
    return (input_grad.astype(jnp.bfloat16), up_grad, down_grad, gain_grad)


def solution(mesh):
    placed = (P(("dp", "mp"), None), P(), P(None, "mp"), P("mp", None), P(("dp", "mp"), None))
    return jax.shard_map(
        per_device,
        mesh=mesh,
        in_specs=placed,
        out_specs=(P(("dp", "mp"), None), P("dp", "mp"), P("mp", "dp"), P()),
        check_vma=False,
    )
```

profile of v0, /device:TPU:10, one launch (start us, length us, event | category | flops | bytes accessed | tf_op | source)
XLA Modules:
  0.0 251.2 jit_solution(14012743861452806159)
XLA Ops:
  7.2 0.0 all-gather.7.cloned.1.call-start
  7.2 1.1 convert_reduce_fusion.2
  8.3 1.2 fusion.19
  9.5 1.7 fusion.13
  11.2 0.0 all-gather.7.cloned.1.call-update
  11.2 0.0 all-gather.5.cloned.1.call-start
  11.3 0.7 all-gather.5.cloned.1.call-update
  12.0 0.0 all-gather.11.cloned.1.call-start
  12.0 25.4 %all-gather.7.cloned.1.call-done = bf16[128,6144]{1,0:T(8,128)(2,1)} async-done(((bf16[16,6144]{1,0:T(8,128)(2,1)}), bf16[128,6144]{1,0:T(8,128)(2,1)}) %all-gather.7.cloned.1.call-update) | async-done | bytes 1572880 | tf_op jit(solution)/shard_map/all_gather | solution.py:26
  37.5 13.1 %multiply_convert_fusion.2 = (bf16[128,2048]{1,0:T(8,128)(2,1)}, f32[128,2048]{1,0:T(8,128)S(1)}) fusion(bf16[128,6144]{1,0:T(8,128)(2,1)} %all-gather.7.cloned.1.call-done, bf16[6144,2048]{1,0:T(8,128)(2,1)} %param.7), kind=kOutput, calls=%fused_computation.15 | convolution fusion | flops 3222536192 | bytes 28311552 | tf_op jit(solution)/shard_map/dot_general | solution.py:29
  50.6 0.0 all-gather.11.cloned.1.call-update
  50.6 0.0 all-gather.9.cloned.1.call-start
  50.6 12.9 %all-gather.5.cloned.1.call-done = bf16[128,6144]{1,0:T(8,128)(2,1)} async-done(((bf16[16,6144]{1,0:T(8,128)(2,1)}), bf16[128,6144]{1,0:T(8,128)(2,1)}) %all-gather.5.cloned.1.call-update) | async-done | bytes 1572880 | tf_op jit(solution)/shard_map/all_gather | solution.py:27
  63.5 14.3 %fusion = bf16[128,2048]{1,0:T(8,128)(2,1)} fusion(bf16[128,6144]{1,0:T(8,128)(2,1)} %all-gather.5.cloned.1.call-done, bf16[2048,6144]{1,0:T(8,128)(2,1)} %param.8, f32[128,2048]{1,0:T(8,128)S(1)} %get-tuple-element.8), kind=kOutput, calls=%fused_computation.7 | convolution fusion | flops 3223846912 | bytes 28311552 | tf_op jit(solution)/shard_map/dot_general | solution.py:31
  77.8 0.0 all-gather.9.cloned.1.call-update
  77.8 0.0 copy-start
  77.9 0.0 reduce-scatter.2.cloned.1.call-start
  77.9 14.4 %fusion.20 = f32[128,6144]{1,0:T(8,128)} fusion(bf16[128,2048]{1,0:T(8,128)(2,1)} %fusion, bf16[6144,2048]{1,0:T(8,128)(2,1)} %param.7), kind=kOutput, calls=%fused_computation.38 | convolution fusion | flops 3221225472 | bytes 28835840 | tf_op jit(solution)/shard_map/dot_general | solution.py:36
  92.4 0.0 copy-start.1
  92.4 0.0 reduce-scatter.2.cloned.1.call-update
  92.4 0.0 copy-done
  92.4 1.6 copy.16
  94.0 2.6 %copy.17 = bf16[128,4,1536]{2,0,1:T(8,128)(2,1)} copy(bf16[128,4,1536]{0,2,1:T(8,128)(2,1)} %bitcast.18) | data formatting | bytes 3145728 | tf_op jit(solution)/shard_map/all_to_all | solution.py:55
  96.5 4.2 %all-to-all-start.1 = ((bf16[128,4,1536]{2,0,1:T(8,128)(2,1)}), bf16[128,4,1536]{2,0,1:T(8,128)(2,1)S(1)}, u32[]{:S(2)}, u32[]{:S(2)}) async-start(bf16[128,4,1536]{2,0,1:T(8,128)(2,1)} %copy.17), calls=%async_computation.2 | async-start | bytes 3145728 | tf_op jit(solution)/shard_map/all_to_all | solution.py:55
  100.7 0.0 copy-done.1
  100.7 1.6 copy.20
  102.3 23.3 %all-to-all-done.1 = bf16[128,4,1536]{2,0,1:T(8,128)(2,1)S(1)} async-done(((bf16[128,4,1536]{2,0,1:T(8,128)(2,1)}), bf16[128,4,1536]{2,0,1:T(8,128)(2,1)S(1)}, u32[]{:S(2)}, u32[]{:S(2)}) %all-to-all-start.1) | async-done | bytes 1572896 | tf_op jit(solution)/shard_map/all_to_all | solution.py:55
  125.6 4.1 %all-to-all-start = ((bf16[128,4,1536]{0,2,1:T(8,128)(2,1)}), bf16[128,4,1536]{0,2,1:T(8,128)(2,1)S(1)}, u32[]{:S(2)}, u32[]{:S(2)}) async-start(bf16[128,4,1536]{0,2,1:T(8,128)(2,1)} %bitcast), calls=%async_computation.1 | async-start | bytes 3145728 | tf_op jit(solution)/shard_map/all_to_all | solution.py:54
  129.7 0.0 all-gather.11.cloned.1.call-done
  129.7 14.2 %convert_reduce_fusion = f32[2048,1536]{1,0:T(8,128)} fusion(bf16[4,128,2048]{2,1,0:T(8,128)(2,1)} %bitcast.19, bf16[128,4,1536]{2,0,1:T(8,128)(2,1)S(1)} %all-to-all-done.1), kind=kOutput, calls=%fused_computation | convolution fusion | flops 3255828480 | bytes 16252928 | tf_op jit(solution)/shard_map/rtf,rtk->rfk/dot_general | solution.py:68
  143.9 15.4 %all-to-all-done = bf16[128,4,1536]{0,2,1:T(8,128)(2,1)S(1)} async-done(((bf16[128,4,1536]{0,2,1:T(8,128)(2,1)}), bf16[128,4,1536]{0,2,1:T(8,128)(2,1)S(1)}, u32[]{:S(2)}, u32[]{:S(2)}) %all-to-all-start) | async-done | bytes 1572896 | tf_op jit(solution)/shard_map/all_to_all | solution.py:54
  159.3 0.0 all-gather.9.cloned.1.call-done
  159.3 14.0 %convert_reduce_fusion.1 = f32[1536,2048]{1,0:T(8,128)} fusion(bf16[4,128,2048]{2,1,0:T(8,128)(2,1)} %bitcast.20, bf16[128,4,1536]{0,2,1:T(8,128)(2,1)S(1)} %all-to-all-done), kind=kOutput, calls=%fused_computation.1 | convolution fusion | flops 3255828480 | bytes 16252928 | tf_op jit(solution)/shard_map/rtk,rtf->rkf/dot_general | solution.py:65
  173.3 9.2 %multiply_convert_fusion = bf16[2048,1536]{1,0:T(8,128)(2,1)} fusion(f32[2048,1536]{1,0:T(8,128)} %convert_reduce_fusion), kind=kLoop, calls=%fused_computation.4 | loop fusion | flops 6291456 | bytes 18874368 | tf_op jit(solution)/shard_map/convert_element_type | solution.py:74
  182.4 0.0 copy-start.2
  182.4 0.0 copy-start.3
  182.4 9.3 %multiply_convert_fusion.1 = bf16[1536,2048]{1,0:T(8,128)(2,1)} fusion(f32[1536,2048]{1,0:T(8,128)} %convert_reduce_fusion.1), kind=kLoop, calls=%fused_computation.5 | loop fusion | flops 6291456 | bytes 18874368 | tf_op jit(solution)/shard_map/convert_element_type | solution.py:73
  191.7 4.7 %reduce-scatter.2.cloned.1.call-done = f32[16,6144]{1,0:T(8,128)} async-done(((f32[128,6144]{1,0:T(8,128)}), f32[16,6144]{1,0:T(8,128)}) %reduce-scatter.2.cloned.1.call-update) | async-done | bytes 393232 | tf_op jit(solution)/shard_map/reduce_scatter | solution.py:35
  196.5 0.0 copy-done.2
  196.5 0.0 copy-done.3
  196.5 1.3 fusion.18
  197.8 44.4 %psum.7 = f32[6144]{0:T(1024)S(1)} all-reduce(f32[6144]{0:T(1024)S(1)} %get-tuple-element.4), channel_id=1, replica_groups=mesh['dp'=4,'mp'=8] {'dp','mp'}, use_global_device_ids=true, to_apply=%region_8.0 | all-reduce | flops 6144 | bytes 49152 | tf_op jit(solution)/shard_map/psum | solution.py:46
  242.2 0.6 broadcast_multiply_fusion
  242.8 1.8 fusion.17
  (3 shorter events, 0.0 us)
Async XLA Ops:
  7.2 30.3 %all-gather.7.cloned.1.call-start = ((), (), s32[]{:S(2)}) async-start(), calls=%async_computation.4 | async-start | bytes 1769472 | tf_op jit(solution)/shard_map/all_gather | solution.py:26
  11.2 52.3 %all-gather.5.cloned.1.call-start = ((), (), s32[]{:S(2)}) async-start(), calls=%async_computation.3 | async-start | bytes 1769472 | tf_op jit(solution)/shard_map/all_gather | solution.py:27
  12.0 117.7 %all-gather.11.cloned.1.call-start = ((), (), s32[]{:S(2)}) async-start(), calls=%async_computation.7 | async-start | bytes 2621440 | tf_op jit(solution)/shard_map/all_gather | solution.py:58
  50.6 108.7 %all-gather.9.cloned.1.call-start = ((), (), s32[]{:S(2)}) async-start(), calls=%async_computation.6 | async-start | bytes 2621440 | tf_op jit(solution)/shard_map/all_gather | solution.py:59
  77.8 14.5 %copy-start = (bf16[128,6144]{1,0:T(8,128)(2,1)S(1)}, bf16[128,6144]{1,0:T(8,128)(2,1)}, u32[]{:S(2)}) copy-start(bf16[128,6144]{1,0:T(8,128)(2,1)} %all-gather.5.cloned.1.call-done) | copy-start | bytes 4718596
  77.9 118.6 %reduce-scatter.2.cloned.1.call-start = ((), (), s32[]{:S(2)}) async-start(), calls=%async_computation.5 | async-start | bytes 3538944 | tf_op jit(solution)/shard_map/reduce_scatter | solution.py:35
  92.4 8.4 %copy-start.1 = (bf16[128,6144]{1,0:T(8,128)(2,1)S(1)}, bf16[128,6144]{1,0:T(8,128)(2,1)}, u32[]{:S(2)}) copy-start(bf16[128,6144]{1,0:T(8,128)(2,1)} %all-gather.7.cloned.1.call-done) | copy-start | bytes 4718596
  96.5 29.0 %all-to-all-start.1 = ((bf16[128,4,1536]{2,0,1:T(8,128)(2,1)}), bf16[128,4,1536]{2,0,1:T(8,128)(2,1)S(1)}, u32[]{:S(2)}, u32[]{:S(2)}) async-start(bf16[128,4,1536]{2,0,1:T(8,128)(2,1)} %copy.17), calls=%async_computation.2 | async-start | bytes 3145728 | tf_op jit(solution)/shard_map/all_to_all | solution.py:55
  125.6 33.7 %all-to-all-start = ((bf16[128,4,1536]{0,2,1:T(8,128)(2,1)}), bf16[128,4,1536]{0,2,1:T(8,128)(2,1)S(1)}, u32[]{:S(2)}, u32[]{:S(2)}) async-start(bf16[128,4,1536]{0,2,1:T(8,128)(2,1)} %bitcast), calls=%async_computation.1 | async-start | bytes 3145728 | tf_op jit(solution)/shard_map/all_to_all | solution.py:54
  182.4 14.0 %copy-start.2 = (bf16[16,6144]{1,0:T(8,128)(2,1)S(1)}, bf16[16,6144]{1,0:T(8,128)(2,1)}, u32[]{:S(2)}) copy-start(bf16[16,6144]{1,0:T(8,128)(2,1)} %param.5) | copy-start | bytes 589828
  182.4 14.0 %copy-start.3 = (f32[6144]{0:T(1024)S(1)}, f32[6144]{0:T(1024)}, u32[]{:S(2)}) copy-start(f32[6144]{0:T(1024)} %param.6) | copy-start | bytes 73732
Sparse Core Ops, SparseCore 0:
  11.4 26.0 all-gather.6
  39.1 24.3 all-gather.4
  65.4 34.6 all-gather.10
  101.8 52.6 all-gather.8
  156.6 39.8 reduce-scatter.1
where the time goes:
time: 252 us; the launch traced here: 251 us
  waiting for transfers between devices  82.5 us (33%)
  matrix products  69.9 us (28%)
  blocking collectives  44.4 us (18%)
  other arithmetic  26.2 us (10%)
  between operations  13.8 us (5%)
  starting transfers between devices  8.55 us (3%)
  local copies, waits for them, and re-layouts  5.71 us (2%)
    psum x1, blocking collectives, per_device(): lax.psum(jnp.sum(norm_grad * x_hat, axis=0), ('dp', 'mp')) * factor  44.4 us
    all_gather x1, waiting for transfers between devices, per_device(): lax.all_gather(normed, 'mp', axis=0, tiled=True)  25.4 us
    all_to_all x1, waiting for transfers between devices, per_device(): lax.all_to_all(cotan_all, 'dp', split_axis=1, concat_axis=0, tiled=True)  23.3 us
    all_to_all x1, waiting for transfers between devices, per_device(): lax.all_to_all(normed_all, 'dp', split_axis=1, concat_axis=0, tiled=True)  15.4 us
    dot_general x1, matrix products, per_device(): lax.dot_general(pre_grad, up_weight, (((1,), (1,)), ((), ())), preferred_...  14.4 us
    dot_general x1, matrix products, per_device(): lax.dot_general(cotan_all, down_weight, (((1,), (1,)), ((), ())), preferr...  14.3 us
    dot_general x1, matrix products, per_device(): jnp.einsum('rtf,rtk->rfk', stacked(hidden_all), stacked(cotan_cols), pref...  14.2 us
    dot_general x1, matrix products, per_device(): jnp.einsum('rtk,rtf->rkf', stacked(normed_cols), stacked(pre_all), prefer...  14 us
  transfers between devices with their start and end apart: 7, of which 5 were waited for; matrix products, arithmetic and copies ran while one was open for 37% of the time, Pallas kernels for 0%

commit v1 on v0

--- a/solution.py
+++ b/solution.py
@@ -3,6 +3,18 @@
 import jax.numpy as jnp
 from jax import lax
 from jax.sharding import PartitionSpec as P
+
+
+def doubled_up(x, axis, dim):
+    ways, here = (lax.axis_size(axis), lax.axis_index(axis))
+    grown, reach = (x, 1)
+    while reach < ways:
+        theirs = lax.ppermute(grown, axis, [(d, d ^ reach) for d in range(ways)])
+        mine_first = jnp.concatenate([grown, theirs], axis=dim)
+        theirs_first = jnp.concatenate([theirs, grown], axis=dim)
+        grown = jnp.where(here & reach == 0, mine_first, theirs_first)
+        reach = 2 * reach
+    return grown
 
 
 def gelu_value(preact):
@@ -24,7 +36,7 @@
     normed = (x_hat * norm_gain).astype(jnp.bfloat16)
     normed_all, cotan_all = (
         lax.all_gather(normed, "mp", axis=0, tiled=True),
-        lax.all_gather(out_grad, "mp", axis=0, tiled=True),
+        doubled_up(out_grad, "mp", 0),
     )
     preact = jnp.dot(normed_all, up_weight, preferred_element_type=jnp.float32)
     hidden = gelu_value(preact).astype(jnp.bfloat16)

time: 252 us -> 268 us (1.063)
  waiting for transfers between devices: 82.5 us -> 94.3 us
  other arithmetic: 26.2 us -> 30.2 us
  matrix products: 69.9 us -> 73.8 us
  local copies, waits for them, and re-layouts: 5.71 us -> 2.45 us
  blocking collectives: 44.4 us -> 41.6 us
    ppermute x0 -> x3, waiting for transfers between devices: none -> 35.8 us  [doubled_up(): theirs = lax.ppermute(grown, axis, [(d, d ^ reach) for d in range(ways)])]
    all_gather x1 -> x0, waiting for transfers between devices: 12.9 us -> none  [per_device(): lax.all_gather(out_grad, 'mp', axis=0, tiled=True)]
    all_to_all x1, waiting for transfers between devices: 15.4 us -> 4.09 us  [per_device(): lax.all_to_all(normed_all, 'dp', split_axis=1, concat_axis=0, tiled=True)]
    all_to_all x1, waiting for transfers between devices: 23.3 us -> 28.6 us  [per_device(): lax.all_to_all(cotan_all, 'dp', split_axis=1, concat_axis=0, tiled=True)]
    reduce_scatter x1, waiting for transfers between devices: 4.71 us -> 0.01 us  [per_device(): lax.psum_scatter(lax.dot_general(pre_grad, up_weight, (((1,), (1,)), ((),...]
    select_n x0 -> x5, other arithmetic: none -> 4.13 us  [doubled_up(): grown = jnp.where(here & reach == 0, mine_first, theirs_first)]
    dot_general x1, matrix products: 14.3 us -> 17.8 us  [per_device(): lax.dot_general(cotan_all, down_weight, (((1,), (1,)), ((), ())), preferr...]
    psum x1, blocking collectives: 44.4 us -> 41.6 us  [per_device(): lax.psum(jnp.sum(norm_grad * x_hat, axis=0), ('dp', 'mp')) * factor]
  transfers between devices with their start and end apart: 7 -> 9, of which waited for: 5 -> 5; matrix products, arithmetic and copies ran while one was open for 37% -> 37% of each run, Pallas kernels for 0% -> 0%
where the time goes in v1:
time: 268 us; the launch traced here: 267 us
  waiting for transfers between devices  94.3 us (35%)
  matrix products  73.8 us (28%)
  blocking collectives  41.6 us (16%)
  other arithmetic  30.2 us (11%)
  between operations  13.9 us (5%)
  starting transfers between devices  11.1 us (4%)
    psum x1, blocking collectives, per_device(): lax.psum(jnp.sum(norm_grad * x_hat, axis=0), ('dp', 'mp')) * factor  41.6 us
    ppermute x3, waiting for transfers between devices, doubled_up(): theirs = lax.ppermute(grown, axis, [(d, d ^ reach) for d in range(ways)])  35.8 us
    all_to_all x1, waiting for transfers between devices, per_device(): lax.all_to_all(cotan_all, 'dp', split_axis=1, concat_axis=0, tiled=True)  28.6 us
    all_gather x1, waiting for transfers between devices, per_device(): lax.all_gather(normed, 'mp', axis=0, tiled=True)  25.6 us
    dot_general x1, matrix products, per_device(): lax.dot_general(cotan_all, down_weight, (((1,), (1,)), ((), ())), preferr...  17.8 us
    dot_general x1, matrix products, per_device(): lax.dot_general(pre_grad, up_weight, (((1,), (1,)), ((), ())), preferred_...  14.9 us
    dot_general x1, matrix products, per_device(): jnp.einsum('rtf,rtk->rfk', stacked(hidden_all), stacked(cotan_cols), pref...  14.2 us
    dot_general x1, matrix products, per_device(): jnp.einsum('rtk,rtf->rkf', stacked(normed_cols), stacked(pre_all), prefer...  14 us
  transfers between devices with their start and end apart: 9, of which 5 were waited for; matrix products, arithmetic and copies ran while one was open for 37% of the time, Pallas kernels for 0%

profile of v1, /device:TPU:10, one launch (start us, length us, event | category | flops | bytes accessed | tf_op | source)
XLA Modules:
  0.0 267.3 jit_solution(12098505955193288882)
XLA Ops:
  7.2 0.0 all-gather.4.cloned.1.call-start
  7.2 1.1 convert_reduce_fusion.2
  8.3 1.2 fusion.25
  9.5 1.7 fusion.19
  11.2 0.0 all-gather.4.cloned.1.call-update
  11.2 0.0 all-gather.8.cloned.1.call-start
  11.3 0.1 collective-permute-start
  11.4 1.6 collective-permute-done
  13.0 1.1 maximum_select_fusion.5
  14.1 0.5 collective-permute-start.1
  14.6 25.6 %all-gather.4.cloned.1.call-done = bf16[128,6144]{1,0:T(8,128)(2,1)} async-done(((bf16[16,6144]{1,0:T(8,128)(2,1)}), bf16[128,6144]{1,0:T(8,128)(2,1)}) %all-gather.4.cloned.1.call-update) | async-done | bytes 1572880 | tf_op jit(solution)/shard_map/all_gather | solution.py:38
  40.3 13.0 %multiply_convert_fusion.2 = (bf16[128,2048]{1,0:T(8,128)(2,1)}, f32[128,2048]{1,0:T(8,128)S(1)}) fusion(bf16[128,6144]{1,0:T(8,128)(2,1)} %all-gather.4.cloned.1.call-done, bf16[6144,2048]{1,0:T(8,128)(2,1)} %param.7), kind=kOutput, calls=%fused_computation.23 | convolution fusion | flops 3222536192 | bytes 28311552 | tf_op jit(solution)/shard_map/dot_general | solution.py:41
  53.2 0.0 all-gather.8.cloned.1.call-update
  53.3 0.0 all-gather.6.cloned.1.call-start
  53.3 0.0 collective-permute-done.1
  53.3 1.0 maximum_select_fusion.3
  54.3 1.8 collective-permute-start.2
  56.2 34.2 %collective-permute-done.2 = bf16[64,6144]{1,0:T(8,128)(2,1)S(1)} collective-permute-done((bf16[64,6144]{1,0:T(8,128)(2,1)}, bf16[64,6144]{1,0:T(8,128)(2,1)S(1)}, u32[]{:S(2)}, u32[]{:S(2)}) %collective-permute-start.2) | collective-permute-done | bytes 786464 | tf_op jit(solution)/shard_map/ppermute | solution.py:12
  90.4 0.0 copy-start.3
  90.4 17.8 %fusion = bf16[128,2048]{1,0:T(8,128)(2,1)} fusion(bf16[2048,6144]{1,0:T(8,128)(2,1)} %param.8, bf16[64,6144]{1,0:T(8,128)(2,1)S(1)} %collective-permute-done.2, bf16[64,6144]{1,0:T(8,128)(2,1)} %maximum_select_fusion.3, pred[]{:T(512)S(6)} %eq.9, f32[128,2048]{1,0:T(8,128)S(1)} %get-tuple-element.8), kind=kOutput, calls=%fused_computation.7 | convolution fusion | flops 3230924800 | bytes 28311552 | tf_op jit(solution)/shard_map/dot_general | solution.py:43
  108.2 0.0 all-gather.6.cloned.1.call-update
  108.2 0.0 reduce-scatter.2.cloned.1.call-start
  108.3 0.0 copy-done.3
  108.3 0.1 maximum_select_fusion.6
  108.4 0.0 copy-start.2
  108.5 0.2 maximum_select_fusion.4
  108.6 0.1 copy.31
  108.7 0.8 copy-done.2
  109.5 14.9 %fusion.27 = f32[128,6144]{1,0:T(8,128)} fusion(bf16[128,2048]{1,0:T(8,128)(2,1)S(1)} %copy-done.2, bf16[6144,2048]{1,0:T(8,128)(2,1)} %param.7), kind=kOutput, calls=%fused_computation.55 | convolution fusion | flops 3221225472 | bytes 28835840 | tf_op jit(solution)/shard_map/dot_general | solution.py:48
  124.3 0.0 reduce-scatter.2.cloned.1.call-update
  124.3 1.8 maximum_select_fusion.2
  126.1 0.0 copy-start
  126.1 4.4 %all-to-all-start.1 = ((bf16[128,4,1536]{2,0,1:T(8,128)(2,1)}), bf16[128,4,1536]{2,0,1:T(8,128)(2,1)S(1)}, u32[]{:S(2)}, u32[]{:S(2)}) async-start(bf16[128,4,1536]{2,0,1:T(8,128)(2,1)} %maximum_select_fusion.2), calls=%async_computation.2 | async-start | bytes 3145728 | tf_op jit(solution)/shard_map/all_to_all | solution.py:67
  130.5 0.0 copy-done
  130.5 1.6 copy.22
  132.1 28.6 %all-to-all-done.1 = bf16[128,4,1536]{2,0,1:T(8,128)(2,1)S(1)} async-done(((bf16[128,4,1536]{2,0,1:T(8,128)(2,1)}), bf16[128,4,1536]{2,0,1:T(8,128)(2,1)S(1)}, u32[]{:S(2)}, u32[]{:S(2)}) %all-to-all-start.1) | async-done | bytes 1572896 | tf_op jit(solution)/shard_map/all_to_all | solution.py:67
  160.7 4.1 %all-to-all-start = ((bf16[128,4,1536]{0,2,1:T(8,128)(2,1)}), bf16[128,4,1536]{0,2,1:T(8,128)(2,1)S(1)}, u32[]{:S(2)}, u32[]{:S(2)}) async-start(bf16[128,4,1536]{0,2,1:T(8,128)(2,1)} %bitcast), calls=%async_computation.1 | async-start | bytes 3145728 | tf_op jit(solution)/shard_map/all_to_all | solution.py:66
  164.8 0.0 all-gather.8.cloned.1.call-done
  164.8 14.2 %convert_reduce_fusion = f32[2048,1536]{1,0:T(8,128)} fusion(bf16[4,128,2048]{2,1,0:T(8,128)(2,1)} %bitcast.33, bf16[128,4,1536]{2,0,1:T(8,128)(2,1)S(1)} %all-to-all-done.1), kind=kOutput, calls=%fused_computation | convolution fusion | flops 3255828480 | bytes 16252928 | tf_op jit(solution)/shard_map/rtf,rtk->rfk/dot_general | solution.py:80
  179.0 4.1 %all-to-all-done = bf16[128,4,1536]{0,2,1:T(8,128)(2,1)S(1)} async-done(((bf16[128,4,1536]{0,2,1:T(8,128)(2,1)}), bf16[128,4,1536]{0,2,1:T(8,128)(2,1)S(1)}, u32[]{:S(2)}, u32[]{:S(2)}) %all-to-all-start) | async-done | bytes 1572896 | tf_op jit(solution)/shard_map/all_to_all | solution.py:66
  183.1 0.0 all-gather.6.cloned.1.call-done
  183.1 14.0 %convert_reduce_fusion.1 = f32[1536,2048]{1,0:T(8,128)} fusion(bf16[4,128,2048]{2,1,0:T(8,128)(2,1)} %bitcast.34, bf16[128,4,1536]{0,2,1:T(8,128)(2,1)S(1)} %all-to-all-done), kind=kOutput, calls=%fused_computation.1 | convolution fusion | flops 3255828480 | bytes 16252928 | tf_op jit(solution)/shard_map/rtk,rtf->rkf/dot_general | solution.py:77
  197.1 9.2 %multiply_convert_fusion.1 = bf16[1536,2048]{1,0:T(8,128)(2,1)} fusion(f32[1536,2048]{1,0:T(8,128)} %convert_reduce_fusion.1), kind=kLoop, calls=%fused_computation.5 | loop fusion | flops 6291456 | bytes 18874368 | tf_op jit(solution)/shard_map/convert_element_type | solution.py:85
  206.3 0.0 copy-start.1
  206.3 0.0 copy-start.4
  206.3 9.0 %multiply_convert_fusion = bf16[2048,1536]{1,0:T(8,128)(2,1)} fusion(f32[2048,1536]{1,0:T(8,128)} %convert_reduce_fusion), kind=kLoop, calls=%fused_computation.4 | loop fusion | flops 6291456 | bytes 18874368 | tf_op jit(solution)/shard_map/convert_element_type | solution.py:86
  215.4 0.0 reduce-scatter.2.cloned.1.call-done
  215.4 0.0 copy-done.1
  215.4 0.0 copy-done.4
  215.4 1.3 fusion.24
  216.7 41.6 %psum.7 = f32[6144]{0:T(1024)S(1)} all-reduce(f32[6144]{0:T(1024)S(1)} %get-tuple-element.4), channel_id=1, replica_groups=mesh['dp'=4,'mp'=8] {'dp','mp'}, use_global_device_ids=true, to_apply=%region_8.9 | all-reduce | flops 6144 | bytes 49152 | tf_op jit(solution)/shard_map/psum | solution.py:58
  258.3 0.6 broadcast_multiply_fusion
  258.9 1.8 fusion.23
  (6 shorter events, 0.1 us)
Async XLA Ops:
  7.2 33.1 %all-gather.4.cloned.1.call-start = ((), (), s32[]{:S(2)}) async-start(), calls=%async_computation.3 | async-start | bytes 1769472 | tf_op jit(solution)/shard_map/all_gather | solution.py:38
  11.2 153.6 %all-gather.8.cloned.1.call-start = ((), (), s32[]{:S(2)}) async-start(), calls=%async_computation.6 | async-start | bytes 2621440 | tf_op jit(solution)/shard_map/all_gather | solution.py:70
  11.3 1.7 collective-permute-start
  14.1 39.2 %collective-permute-start.1 = (bf16[32,6144]{1,0:T(8,128)(2,1)S(1)}, bf16[32,6144]{1,0:T(8,128)(2,1)S(1)}, u32[]{:S(2)}, u32[]{:S(2)}) collective-permute-start(bf16[32,6144]{1,0:T(8,128)(2,1)S(1)} %maximum_select_fusion.5), channel_id=1, source_target_pairs={{0,2},{1,3},{2,0},{3,1},{4,6},{5,7},{6,4},{7,5},{8,10},{9,11},{10,... | collective-permute-start | bytes 1179656 | tf_op jit(solution)/shard_map/ppermute | solution.py:12
  53.3 129.8 %all-gather.6.cloned.1.call-start = ((), (), s32[]{:S(2)}) async-start(), calls=%async_computation.5 | async-start | bytes 2621440 | tf_op jit(solution)/shard_map/all_gather | solution.py:71
  54.3 36.1 %collective-permute-start.2 = (bf16[64,6144]{1,0:T(8,128)(2,1)}, bf16[64,6144]{1,0:T(8,128)(2,1)S(1)}, u32[]{:S(2)}, u32[]{:S(2)}) collective-permute-start(bf16[64,6144]{1,0:T(8,128)(2,1)} %maximum_select_fusion.3), channel_id=1, source_target_pairs={{0,4},{1,5},{2,6},{3,7},{4,0},{5,1},{6,2},{7,3},{8,12},{9,13},{10,... | collective-permute-start | bytes 2359304 | tf_op jit(solution)/shard_map/ppermute | solution.py:12
  90.4 17.9 %copy-start.3 = (bf16[16,6144]{1,0:T(8,128)(2,1)S(1)}, bf16[16,6144]{1,0:T(8,128)(2,1)}, u32[]{:S(2)}) copy-start(bf16[16,6144]{1,0:T(8,128)(2,1)} %param.9) | copy-start | bytes 589828
  108.2 107.1 %reduce-scatter.2.cloned.1.call-start = ((), (), s32[]{:S(2)}) async-start(), calls=%async_computation.4 | async-start | bytes 3538944 | tf_op jit(solution)/shard_map/reduce_scatter | solution.py:47
  108.4 1.0 copy-start.2
  126.1 4.4 %copy-start = (bf16[128,6144]{1,0:T(8,128)(2,1)S(1)}, bf16[128,6144]{1,0:T(8,128)(2,1)}, u32[]{:S(2)}) copy-start(bf16[128,6144]{1,0:T(8,128)(2,1)} %all-gather.4.cloned.1.call-done) | copy-start | bytes 4718596
  126.1 34.6 %all-to-all-start.1 = ((bf16[128,4,1536]{2,0,1:T(8,128)(2,1)}), bf16[128,4,1536]{2,0,1:T(8,128)(2,1)S(1)}, u32[]{:S(2)}, u32[]{:S(2)}) async-start(bf16[128,4,1536]{2,0,1:T(8,128)(2,1)} %maximum_select_fusion.2), calls=%async_computation.2 | async-start | bytes 3145728 | tf_op jit(solution)/shard_map/all_to_all | solution.py:67
  160.7 22.4 %all-to-all-start = ((bf16[128,4,1536]{0,2,1:T(8,128)(2,1)}), bf16[128,4,1536]{0,2,1:T(8,128)(2,1)S(1)}, u32[]{:S(2)}, u32[]{:S(2)}) async-start(bf16[128,4,1536]{0,2,1:T(8,128)(2,1)} %bitcast), calls=%async_computation.1 | async-start | bytes 3145728 | tf_op jit(solution)/shard_map/all_to_all | solution.py:66
  206.3 9.1 %copy-start.1 = (bf16[16,6144]{1,0:T(8,128)(2,1)S(1)}, bf16[16,6144]{1,0:T(8,128)(2,1)}, u32[]{:S(2)}) copy-start(bf16[16,6144]{1,0:T(8,128)(2,1)} %param.5) | copy-start | bytes 589828
  206.3 9.1 %copy-start.4 = (f32[6144]{0:T(1024)S(1)}, f32[6144]{0:T(1024)}, u32[]{:S(2)}) copy-start(f32[6144]{0:T(1024)} %param.6) | copy-start | bytes 73732
Sparse Core Ops, SparseCore 0:
  11.4 28.8 all-gather.3
  53.4 35.5 all-gather.7
  108.4 48.3 all-gather.5
  158.9 41.2 reduce-scatter.1
